TPU v7x, 32 devices: a whole 2x2x4 slice. The times are simulated.
32 devices in a mesh: rows: 16 (over z, y, x), width: 2 (over core).
Axes of the slice: x: 2, y: 2, z: 4, core: 2. Of those that a mesh axis runs over, the one named last changes fastest.
Arguments:
- left_feat: bfloat16 [16, 2048, 256], P('rows', 'width'), may hold values from -28 to 28
- right_feat: bfloat16 [16, 2048, 256], P('rows', 'width'), may hold values from -28 to 28
- refine_weight: bfloat16 [3, 3, 256, 256], replicated, may hold values from -0.125 to 0.125
Outputs:
- disparity: float32 [16, 2048], P('rows', 'width')
- refined: bfloat16 [16, 2048, 256], P('rows', 'width')
All inputs are finite; a program needn't handle non-finite values.
Results may differ from a plain program's by a relative error of at most 0.0049.
Values may be sent and summed in bfloat16 or wider, within the bound.
A program may use at most 64 MiB of HBM per device.

v0:
```python
import math

import jax
import jax.numpy as jnp
from jax import lax
from jax.sharding import PartitionSpec as P

NEG_FILL = -1e30


def extended(value, sides, width):
    for axis, dim in sides:
        size, length = (lax.axis_size(axis), value.shape[dim])
        up = [(i, (i + 1) % size) for i in range(size - 1)]
        down = [(j, i) for i, j in up]
        last = lax.slice_in_dim(value, length - width, length, axis=dim)
        leading = lax.slice_in_dim(value, 0, width, axis=dim)
        before = lax.ppermute(last, axis, up)
        after = lax.ppermute(leading, axis, down)
        value = jnp.concatenate([before, value, after], axis=dim)
    return value


def absorb_block(state_now, query_rows, query_positions, sub_keys, key_positions):
    run_max, run_total, weighted, position_sum = state_now
    score_scale = 1.0 / math.sqrt(query_rows.shape[-1])
    scores = (
        jnp.einsum("rqc,rkc->rqk", query_rows, sub_keys, preferred_element_type=jnp.float32)
        * score_scale
    )
    allowed = (key_positions[None, :] <= query_positions[:, None]) & (key_positions[None, :] >= 0)
    scores = jnp.where(allowed[None], scores, NEG_FILL)
    new_max = jnp.maximum(run_max, scores.max(-1))
    factor = jnp.exp(run_max - new_max)
    weights = jnp.where(allowed[None], jnp.exp(scores - new_max[..., None]), 0.0)
    run_total = run_total * factor + weights.sum(-1)
    weighted = weighted * factor[..., None] + jnp.einsum(
        "rqk,rkc->rqc", weights.astype(jnp.bfloat16), sub_keys, preferred_element_type=jnp.float32
    )
    position_sum = position_sum * factor + (
        weights * key_positions.astype(jnp.float32)[None, None, :]
    ).sum(-1)
    return (new_max, run_total, weighted, position_sum)


def absorb_piece(state_now, query_rows, query_positions, key_piece):
    n_keys = key_piece.shape[1]
    sub_len = math.gcd(n_keys, 512)
    count = n_keys // sub_len
    last_query = query_positions[-1]

    def one_sub(carry_state, sub_index):
        sub_start = sub_index * sub_len
        sub_keys = lax.dynamic_slice_in_dim(key_piece, sub_index * sub_len, sub_len, 1)
        key_positions = sub_start + jnp.arange(sub_len, dtype=jnp.int32)
        result_state = lax.cond(
            sub_start <= last_query,
            lambda inner: absorb_block(inner, query_rows, query_positions, sub_keys, key_positions),
            lambda inner: inner,
            carry_state,
        )
        return (result_state, None)

    result, _ = lax.scan(one_sub, state_now, jnp.arange(count, dtype=jnp.int32))
    return result


def empty_state(rows_here, length, chans):
    return (
        jnp.full((rows_here, length), NEG_FILL, jnp.float32),
        jnp.zeros((rows_here, length), jnp.float32),
        jnp.zeros((rows_here, length, chans), jnp.float32),
        jnp.zeros((rows_here, length), jnp.float32),
    )


def finish_state(state_now, query_positions):
    run_max, run_total, weighted, position_sum = state_now
    matched = (weighted / run_total[..., None]).astype(jnp.bfloat16)
    disparity = query_positions.astype(jnp.float32)[None, :] - position_sum / run_total
    return (matched, disparity)


def body(left_feat, right_feat, refine_weight):
    rows_here, block_len, chans = left_feat.shape
    my_index = lax.axis_index("width")
    offset = my_index * block_len
    query_positions = offset + jnp.arange(block_len, dtype=jnp.int32)
    final_state = absorb_piece(
        empty_state(rows_here, block_len, chans),
        left_feat,
        query_positions,
        lax.all_gather(right_feat, "width", axis=1, tiled=True),
    )
    matched, disparity = finish_state(final_state, query_positions)
    padded = extended(matched, (("rows", 0), ("width", 1)), 1)
    total = jnp.zeros((rows_here * block_len, chans), jnp.float32)
    for tap_row in range(3):
        for tap_col in range(3):
            window = padded[tap_row : tap_row + rows_here, tap_col : tap_col + block_len].reshape(
                -1, chans
            )
            total = total + jnp.dot(
                window, refine_weight[tap_row, tap_col], preferred_element_type=jnp.float32
            )
    refined = total.reshape(rows_here, block_len, chans).astype(jnp.bfloat16)
    return (disparity, refined)


def solution(mesh):
    placed = (P("rows", "width", None), P("rows", "width", None), P())
    return jax.shard_map(
        body,
        mesh=mesh,
        in_specs=placed,
        out_specs=(P("rows", "width"), P("rows", "width", None)),
        check_vma=False,
    )
```

profile of v0, /device:TPU:0, one launch (start us, length us, event | category | flops | bytes accessed | tf_op | source)
XLA Modules:
  0.0 81.7 jit_solution(14287782797490262223)
XLA Ops:
  7.2 0.0 all-gather.2.cloned.1.call-start
  7.2 0.7 all-gather.2.cloned.1.call-update
  7.9 0.6 slice.60
  8.5 12.8 %all-gather.2.cloned.1.call-done = bf16[1,2048,256]{2,1,0:T(8,128)(2,1)} async-done(((bf16[1,1024,256]{2,1,0:T(8,128)(2,1)}), bf16[1,2048,256]{2,1,0:T(8,128)(2,1)}) %all-gather.2.cloned.1.call-update) | async-done | bytes 1048592 | tf_op jit(solution)/shard_map/all_gather | solution.py:93
  21.3 0.1 broadcast_in_dim.20
  21.4 0.0 copy-start
  21.4 17.5 %while.17 = (s32[]{:T(128)}, f32[1,1024]{1,0:T(1,128)S(1)}, f32[1,1024]{1,0:T(1,128)S(1)}, f32[1,1024,256]{2,1,0:T(8,128)S(1)}, f32[1,1024]{1,0:T(1,128)S(1)}, /...) while((s32[]{:T(128)}, f32[1,1024]{1,0:T(1,128)S(1)}, ...), condition=%wide.region_6.7_spmd.clone, body=%wide.region_0.6_spmd.clone.sunk | while | flops 546313728 | bytes 9568613 | solution.py:64
  21.4 0.6 dynamic_slice.24
  23.3 4.9 %conditional.3 = ((f32[1,1024]{1,0:T(1,128)S(1)}, f32[1,1024]{1,0:T(1,128)S(1)}, f32[1,1024,256]{2,1,0:T(8,128)S(1)}, f32[1,1024]{1,0:T(1,128)S(1)})) conditional(s32[]{:T(128)} %convert_element_type.47, (f32[1,1024]{1,0:T(1,128)S(1)}, f32[1,1024]{1,0:T(1,128)S(1)}, f32[1,1024,256]{2,1,0:T(8,128)S(1)}, f32[1,1024]{1,0:T(1,128)S(1)}) %tuple.47, ...), branch_computations={%region_1.1_spmd, %region_2.5_spmd} | conditional | flops 546313728 | bytes 9562202 | solution.py:56
  23.4 1.8 %fusion.85 = (f32[1024]{0:T(1024)S(1)}, f32[1024,512]{0,1:T(8,128)S(1)}) fusion(bf16[1,1024,256]{2,1,0:T(8,128)(2,1)} %get-tuple-element.134, bf16[1,2048,256]{2,1,0:T(8,128)(2,1)} %get-tuple-element.133, s32[]{:T(128)S(6)} %select_n.16, pred[512]{0:T(512)(128)(4,1)S(1)} %broadcast_compare_fusion, s32[1024]{0:T(1024)S(1)} %broadcast_add_fusion, ...), kind=kOutput, calls=%fused_computation.111 | convolution fusion | flops 271055872 | bytes 2894340 | tf_op jit(solution)/shard_map/while/body/eval_jaxpr/cond/branch_1_fun/rqc,rkc->rqk/dot_general | solution.py:28
  25.2 0.8 multiply_reduce_fusion
  26.1 2.1 %fusion.2 = f32[1,1024,256]{2,1,0:T(8,128)S(1)} fusion(f32[1,1024,256]{2,1,0:T(8,128)S(1)} %get-tuple-element.136, f32[1024]{0:T(1024)S(1)} %bitcast.88, bf16[1,2048,256]{2,1,0:T(8,128)(2,1)} %get-tuple-element.133, s32[]{:T(128)S(6)} %select_n.16, f32[1024,512]{0,1:T(8,128)S(1)} %get-tuple-element.218, f32[1024]{0:T(1024)S(1)} %bitcast.85, ...), kind=kOutput, calls=%fused_computation.6 | convolution fusion | flops 271581184 | bytes 4471300 | tf_op jit(solution)/shard_map/while/body/eval_jaxpr/cond/branch_1_fun/rqk,rkc->rqc/dot_general | solution.py:37
  28.2 0.6 dynamic_slice.24
  30.1 4.9 %conditional.3 = ((f32[1,1024]{1,0:T(1,128)S(1)}, f32[1,1024]{1,0:T(1,128)S(1)}, f32[1,1024,256]{2,1,0:T(8,128)S(1)}, f32[1,1024]{1,0:T(1,128)S(1)})) conditional(s32[]{:T(128)} %convert_element_type.47, (f32[1,1024]{1,0:T(1,128)S(1)}, f32[1,1024]{1,0:T(1,128)S(1)}, f32[1,1024,256]{2,1,0:T(8,128)S(1)}, f32[1,1024]{1,0:T(1,128)S(1)}) %tuple.47, ...), branch_computations={%region_1.1_spmd, %region_2.5_spmd} | conditional | flops 546313728 | bytes 9562202 | solution.py:56
  30.2 1.8 %fusion.85 = (f32[1024]{0:T(1024)S(1)}, f32[1024,512]{0,1:T(8,128)S(1)}) fusion(bf16[1,1024,256]{2,1,0:T(8,128)(2,1)} %get-tuple-element.134, bf16[1,2048,256]{2,1,0:T(8,128)(2,1)} %get-tuple-element.133, s32[]{:T(128)S(6)} %select_n.16, pred[512]{0:T(512)(128)(4,1)S(1)} %broadcast_compare_fusion, s32[1024]{0:T(1024)S(1)} %broadcast_add_fusion, ...), kind=kOutput, calls=%fused_computation.111 | convolution fusion | flops 271055872 | bytes 2894340 | tf_op jit(solution)/shard_map/while/body/eval_jaxpr/cond/branch_1_fun/rqc,rkc->rqk/dot_general | solution.py:28
  32.0 0.8 multiply_reduce_fusion
  32.9 2.1 %fusion.2 = f32[1,1024,256]{2,1,0:T(8,128)S(1)} fusion(f32[1,1024,256]{2,1,0:T(8,128)S(1)} %get-tuple-element.136, f32[1024]{0:T(1024)S(1)} %bitcast.88, bf16[1,2048,256]{2,1,0:T(8,128)(2,1)} %get-tuple-element.133, s32[]{:T(128)S(6)} %select_n.16, f32[1024,512]{0,1:T(8,128)S(1)} %get-tuple-element.218, f32[1024]{0:T(1024)S(1)} %bitcast.85, ...), kind=kOutput, calls=%fused_computation.6 | convolution fusion | flops 271581184 | bytes 4471300 | tf_op jit(solution)/shard_map/while/body/eval_jaxpr/cond/branch_1_fun/rqk,rkc->rqc/dot_general | solution.py:37
  35.0 0.6 dynamic_slice.24
  37.0 0.6 dynamic_slice.24
  38.9 0.2 divide_convert_fusion
  39.1 3.7 %collective-permute-start = (bf16[1,1024,256]{2,1,0:T(8,128)(2,1)S(1)}, bf16[1,1024,256]{2,1,0:T(8,128)(2,1)S(1)}, u32[]{:S(2)}, u32[]{:S(2)}) collective-permute-start(bf16[1,1024,256]{2,1,0:T(8,128)(2,1)S(1)} %divide_convert_fusion), channel_id=1, source_target_pairs={{0,2},{2,4},{4,6},{6,8},{8,10},{10,12},{12,14},{14,16},{16,18},{18... | collective-permute-start | bytes 1572872 | tf_op jit(solution)/shard_map/ppermute | solution.py:18
  42.8 1.3 %collective-permute-start.1 = (bf16[1,1024,256]{2,1,0:T(8,128)(2,1)S(1)}, bf16[1,1024,256]{2,1,0:T(8,128)(2,1)S(1)}, u32[]{:S(2)}, u32[]{:S(2)}) collective-permute-start(bf16[1,1024,256]{2,1,0:T(8,128)(2,1)S(1)} %divide_convert_fusion), channel_id=1, source_target_pairs={{2,0},{4,2},{6,4},{8,6},{10,8},{12,10},{14,12},{16,14},{18,16},{20... | collective-permute-start | bytes 1572872 | tf_op jit(solution)/shard_map/ppermute | solution.py:19
  44.1 0.6 divide_subtract_fusion
  44.7 0.0 copy-done
  44.7 0.3 fusion.56
  45.0 10.2 %collective-permute-done = bf16[1,1024,256]{2,1,0:T(8,128)(2,1)S(1)} collective-permute-done((bf16[1,1024,256]{2,1,0:T(8,128)(2,1)S(1)}, bf16[1,1024,256]{2,1,0:T(8,128)(2,1)S(1)}, u32[]{:S(2)}, u32[]{:S(2)}) %collective-permute-start) | collective-permute-done | bytes 524320 | tf_op jit(solution)/shard_map/ppermute | solution.py:18
  55.2 3.9 %collective-permute-done.1 = bf16[1,1024,256]{2,1,0:T(8,128)(2,1)S(1)} collective-permute-done((bf16[1,1024,256]{2,1,0:T(8,128)(2,1)S(1)}, bf16[1,1024,256]{2,1,0:T(8,128)(2,1)S(1)}, u32[]{:S(2)}, u32[]{:S(2)}) %collective-permute-start.1) | collective-permute-done | bytes 524320 | tf_op jit(solution)/shard_map/ppermute | solution.py:19
  59.2 1.3 %collective-permute-start.3 = (bf16[3,1,256]{2,1,0:T(2,128)(2,1)S(1)}, bf16[3,1,256]{2,1,0:T(2,128)(2,1)S(1)}, u32[]{:S(2)}, u32[]{:S(2)}) collective-permute-start(bf16[3,1,256]{2,1,0:T(2,128)(2,1)S(1)} %get-tuple-element.220), channel_id=1, source_target_pairs={{1,0},{3,2},{5,4},{7,6},{9,8},{11,10},{13,12},{15,14},{17,16},{19,... | collective-permute-start | bytes 4616 | tf_op jit(solution)/shard_map/ppermute | solution.py:19
  60.5 10.8 %collective-permute-start.2 = (bf16[3,1,256]{2,1,0:T(2,128)(2,1)S(1)}, bf16[3,1,256]{2,1,0:T(2,128)(2,1)S(1)}, u32[]{:S(2)}, u32[]{:S(2)}) collective-permute-start(bf16[3,1,256]{2,1,0:T(2,128)(2,1)S(1)} %get-tuple-element.219), channel_id=1, source_target_pairs={{0,1},{2,3},{4,5},{6,7},{8,9},{10,11},{12,13},{14,15},{16,17},{18,... | collective-permute-start | bytes 4616 | tf_op jit(solution)/shard_map/ppermute | solution.py:18
  71.2 0.3 fusion.58
  71.5 0.3 fusion.54
  71.9 0.2 collective-permute-done.2
  72.1 0.3 fusion.34
  72.4 0.3 fusion.25
  72.7 0.0 collective-permute-done.3
  72.7 0.3 fusion.41
  73.0 0.3 fusion.21
  73.3 0.4 fusion.17
  73.7 1.2 %fusion.19 = bf16[1,1024,256]{2,1,0:T(8,128)(2,1)} fusion(f32[1024,256]{1,0:T(8,128)S(1)} %fusion.21, f32[1024,256]{1,0:T(8,128)S(1)} %fusion.54, f32[1024,256]{1,0:T(8,128)S(1)} %fusion.25, f32[1024,256]{1,0:T(8,128)S(1)} %fusion.17, bf16[3,1,256]{2,1,0:T(2,128)(2,1)S(1)} %collective-permute-done.3, bf16[1,1024,256]{2,1,0:T(8,128)(2,1)S(1)} %collective-permute-done.1, ...), kind=kOutput, calls=%fused_computation.31 | convolution fusion | flops 137625600 | bytes 6425600 | tf_op jit(solution)/shard_map/dot_general | solution.py:103
  (30 shorter events, 0.2 us)
Async XLA Ops:
  7.2 14.1 %all-gather.2.cloned.1.call-start = ((), (), s32[]{:S(2)}) async-start(), calls=%async_computation | async-start | bytes 1572864 | tf_op jit(solution)/shard_map/all_gather | solution.py:93
  21.4 23.3 %copy-start = (bf16[3,3,256,256]{3,2,1,0:T(8,128)(2,1)S(1)}, bf16[3,3,256,256]{3,2,1,0:T(8,128)(2,1)}, u32[]{:S(2)}) copy-start(bf16[3,3,256,256]{3,2,1,0:T(8,128)(2,1)} %param.9) | copy-start | bytes 3538948
  39.1 16.1 %collective-permute-start = (bf16[1,1024,256]{2,1,0:T(8,128)(2,1)S(1)}, bf16[1,1024,256]{2,1,0:T(8,128)(2,1)S(1)}, u32[]{:S(2)}, u32[]{:S(2)}) collective-permute-start(bf16[1,1024,256]{2,1,0:T(8,128)(2,1)S(1)} %divide_convert_fusion), channel_id=1, source_target_pairs={{0,2},{2,4},{4,6},{6,8},{8,10},{10,12},{12,14},{14,16},{16,18},{18... | collective-permute-start | bytes 1572872 | tf_op jit(solution)/shard_map/ppermute | solution.py:18
  42.8 16.4 %collective-permute-start.1 = (bf16[1,1024,256]{2,1,0:T(8,128)(2,1)S(1)}, bf16[1,1024,256]{2,1,0:T(8,128)(2,1)S(1)}, u32[]{:S(2)}, u32[]{:S(2)}) collective-permute-start(bf16[1,1024,256]{2,1,0:T(8,128)(2,1)S(1)} %divide_convert_fusion), channel_id=1, source_target_pairs={{2,0},{4,2},{6,4},{8,6},{10,8},{12,10},{14,12},{16,14},{18,16},{20... | collective-permute-start | bytes 1572872 | tf_op jit(solution)/shard_map/ppermute | solution.py:19
  59.2 13.5 %collective-permute-start.3 = (bf16[3,1,256]{2,1,0:T(2,128)(2,1)S(1)}, bf16[3,1,256]{2,1,0:T(2,128)(2,1)S(1)}, u32[]{:S(2)}, u32[]{:S(2)}) collective-permute-start(bf16[3,1,256]{2,1,0:T(2,128)(2,1)S(1)} %get-tuple-element.220), channel_id=1, source_target_pairs={{1,0},{3,2},{5,4},{7,6},{9,8},{11,10},{13,12},{15,14},{17,16},{19,... | collective-permute-start | bytes 4616 | tf_op jit(solution)/shard_map/ppermute | solution.py:19
  60.5 11.6 %collective-permute-start.2 = (bf16[3,1,256]{2,1,0:T(2,128)(2,1)S(1)}, bf16[3,1,256]{2,1,0:T(2,128)(2,1)S(1)}, u32[]{:S(2)}, u32[]{:S(2)}) collective-permute-start(bf16[3,1,256]{2,1,0:T(2,128)(2,1)S(1)} %get-tuple-element.219), channel_id=1, source_target_pairs={{0,1},{2,3},{4,5},{6,7},{8,9},{10,11},{12,13},{14,15},{16,17},{18,... | collective-permute-start | bytes 4616 | tf_op jit(solution)/shard_map/ppermute | solution.py:18
Sparse Core Ops, SparseCore 0:
  9.5 11.7 all-gather.1
where the time goes:
time: 82.2 us; the launch traced here: 81.7 us
  waiting for transfers between devices  27.8 us (34%)
  starting transfers between devices  17.1 us (21%)
  between operations  14.2 us (17%)
  matrix products  11.5 us (14%)
  loops' own time  5.41 us (7%)
  local copies, waits for them, and re-layouts  3.16 us (4%)
  other arithmetic  2.57 us (3%)
    ppermute x2, starting transfers between devices, extended(): before = lax.ppermute(last, axis, up)  14.4 us
    all_gather x1, waiting for transfers between devices, body(): lax.all_gather(right_feat, 'width', axis=1, tiled=True)  12.8 us
    ppermute x2, waiting for transfers between devices, extended(): before = lax.ppermute(last, axis, up)  10.4 us
    another operation x1, loops' own time, absorb_piece(): result, _ = lax.scan(one_sub, state_now, jnp.arange(count, dtype=jnp.int32))  5.2 us
    dot_general x2, matrix products, absorb_block(): jnp.einsum('rqk,rkc->rqc', weights.astype(jnp.bfloat16), sub_keys, prefer...  4.21 us
    ppermute x2, waiting for transfers between devices, extended(): after = lax.ppermute(leading, axis, down)  3.93 us
    dot_general x9, matrix products, body(): jnp.dot(window, refine_weight[tap_row, tap_col], preferred_element_type=j...  3.71 us
    dot_general x2, matrix products, absorb_block(): jnp.einsum('rqc,rkc->rqk', query_rows, sub_keys, preferred_element_type=j...  3.62 us
  transfers between devices with their start and end apart: 5, of which 4 were waited for; matrix products, arithmetic and copies ran while one was open for 3% of the time, Pallas kernels for 0%

commit v1 on v0

--- a/solution.py
+++ b/solution.py
@@ -1,8 +1,11 @@
+import functools
 import math
 
 import jax
 import jax.numpy as jnp
 from jax import lax
+from jax.experimental import pallas as pl
+from jax.experimental.pallas import tpu as pltpu
 from jax.sharding import PartitionSpec as P
 
 NEG_FILL = -1e30
@@ -107,10 +110,308 @@
     return (disparity, refined)
 
 
+MESH = pl.DeviceIdType.MESH
+EDGE = 16
+LANES = 128
+
+
+def attend(left, keys, scores, own, disp_ref, tile, first_key_tile, size):
+    chans = left.shape[-1]
+    gain = math.log2(math.e) / math.sqrt(chans)
+    n_tiles = first_key_tile + tile + 1
+    rows = pl.ds(tile * size, size)
+    queries = left[rows, :]
+    lane_max = jnp.full((size, LANES), NEG_FILL, jnp.float32)
+    for kt in range(n_tiles):
+        s = lax.dot_general(
+            queries,
+            keys[pl.ds(kt * size, size), :],
+            (((1,), (1,)), ((), ())),
+            preferred_element_type=jnp.float32,
+        )
+        if kt == n_tiles - 1:
+            q_at = lax.broadcasted_iota(jnp.int32, (size, size), 0)
+            k_at = lax.broadcasted_iota(jnp.int32, (size, size), 1)
+            s = jnp.where(k_at <= q_at, s, NEG_FILL)
+        scores[:, pl.ds(kt * size, size)] = s
+        for c in range(0, size, LANES):
+            lane_max = jnp.maximum(lane_max, s[:, c : c + LANES])
+    row_max = jnp.max(lane_max, axis=1, keepdims=True)
+    total = jnp.zeros((size, LANES), jnp.float32)
+    prefix = jnp.zeros((size, LANES), jnp.float32)
+    acc = jnp.zeros((size, chans), jnp.float32)
+    for kt in range(n_tiles):
+        p = jnp.exp2((scores[:, pl.ds(kt * size, size)] - row_max) * gain)
+        for c in range(0, size, LANES):
+            total = total + p[:, c : c + LANES]
+            prefix = prefix + total
+        acc = acc + jnp.dot(
+            p.astype(jnp.bfloat16),
+            keys[pl.ds(kt * size, size), :],
+            preferred_element_type=jnp.float32,
+        )
+    denominator = jnp.sum(total, axis=1, keepdims=True)
+    own[rows, :] = (acc * (1.0 / denominator)).astype(jnp.bfloat16)
+    n_chunks = n_tiles * (size // LANES)
+    lane = lax.broadcasted_iota(jnp.int32, (size, LANES), 1).astype(jnp.float32)
+    position = LANES * (n_chunks * total - prefix) + lane * total
+    total_t = jnp.sum(total.T, axis=0, keepdims=True)
+    position_t = jnp.sum(position.T, axis=0, keepdims=True)
+    at = lax.broadcasted_iota(jnp.int32, (1, size), 1) + (n_tiles - 1) * size
+    disp_ref[:, rows] = at.astype(jnp.float32) - position_t / total_t
+
+
+def kernel(
+    n_rows, size, chunk,
+    left_hbm, right_hbm, weight_hbm,
+    disp_ref, out_ref,
+    left, keys, weight, scores, own, arrived, edges, sums,
+    load_sem, key_sem, x_sem, y_sem, z_sem, edge_sem,
+):
+    length, chans = left.shape
+    n_tiles, n_chunks = length // size, length // chunk
+    r, w = lax.axis_index("rows"), lax.axis_index("width")
+    m = r % 4
+    other_w = 1 - w
+    x_row = r + 1 - 2 * (m % 2)
+    y_row = r + 2 - 4 * (m // 2)
+    outer = (m == 0) | (m == 3)
+    below, above = outer & (r >= 4), outer & (r + 4 < n_rows)
+    z_send = ((m == 0) & (r + 4 < n_rows)) | ((m == 3) & (r >= 4))
+    z_recv = ((m == 0) & (r >= 4)) | ((m == 3) & (r + 4 < n_rows))
+    z_row = jnp.where(m == 0, r + 4, jnp.where(m == 3, r - 4, x_row))
+
+    loads = [
+        pltpu.make_async_copy(left_hbm.at[0], left, load_sem.at[0]),
+        pltpu.make_async_copy(right_hbm.at[0], keys.at[pl.ds(w * length, length)], load_sem.at[1]),
+        pltpu.make_async_copy(weight_hbm, weight, load_sem.at[2]),
+    ]
+    for load in loads:
+        load.start()
+
+    barrier = pltpu.get_barrier_semaphore()
+    for there in ((r, other_w), (x_row, w), (y_row, w)):
+        pl.semaphore_signal(barrier, inc=1, device_id=there, device_id_type=MESH)
+
+    @pl.when(below)
+    def _():
+        pl.semaphore_signal(barrier, inc=1, device_id=(r - 4, w), device_id_type=MESH)
+
+    @pl.when(above)
+    def _():
+        pl.semaphore_signal(barrier, inc=1, device_id=(r + 4, w), device_id_type=MESH)
+
+    pl.semaphore_wait(barrier, 3 + below.astype(jnp.int32) + above.astype(jnp.int32))
+
+    def remote(src, dst, sems, k, row, col):
+        return pltpu.make_async_remote_copy(
+            src_ref=src, dst_ref=dst, send_sem=sems.at[0, k], recv_sem=sems.at[1, k],
+            device_id=(row, col), device_id_type=MESH,
+        )
+
+    def part(k):
+        return pl.ds(pl.multiple_of(k * chunk, chunk), chunk)
+
+    def x_copy(k):
+        return remote(own.at[part(k)], arrived.at[0, part(k)], x_sem, k, x_row, w)
+
+    def y_copy(k):
+        return remote(arrived.at[0, part(k)], arrived.at[1, part(k)], y_sem, k, y_row, w)
+
+    def z_copy(k):
+        return remote(arrived.at[1, part(k)], arrived.at[2, part(k)], z_sem, k, z_row, w)
+
+    edge_at = pl.ds(pl.multiple_of((1 - w) * (length - EDGE), EDGE), EDGE)
+    edge_chunk = (1 - w) * (n_chunks - 1)
+    slot = jnp.where(outer, 2, 1)
+
+    def edge_copy(j):
+        src = own.at[edge_at] if j == 0 else arrived.at[0 if j == 1 else slot, edge_at]
+        return remote(src, edges.at[j], edge_sem, j, r, other_w)
+
+    key_copy = remote(right_hbm.at[0], keys.at[pl.ds(0, length)], key_sem, 0, r, other_w)
+
+    @pl.when(w == 0)
+    def _():
+        key_copy.start()
+
+    for load in loads:
+        load.wait()
+
+    for side in (0, 1):
+
+        @pl.when(w == side)
+        def _():
+            if side == 1:
+                key_copy.wait_recv()
+            for tile in range(n_tiles):
+                attend(left, keys, scores, own, disp_ref, tile, side * n_tiles, size)
+                for k in range(tile * size // chunk, (tile + 1) * size // chunk):
+                    x_copy(k).start()
+
+    edge_copy(0).start()
+
+    @pl.when(jnp.logical_not(z_recv))
+    def _():
+        arrived[2] = jnp.zeros((length, chans), jnp.bfloat16)
+
+    zeros = jnp.zeros((EDGE, chans), jnp.float32)
+    sums[0, pl.ds(0, EDGE), :] = zeros
+    sums[2, pl.ds(EDGE + length, EDGE), :] = zeros
+    x_tap = 2 - 2 * (m % 2)
+    other_tap = 2 - x_tap
+
+    def emit(start, n):
+        before = sums[0, pl.ds(start + EDGE - 8, n + 8), :]
+        after = sums[2, pl.ds(start + EDGE, n + 8), :]
+        total = (
+            pltpu.roll(before, 1, 0)[8:, :]
+            + sums[1, pl.ds(start + EDGE, n), :]
+            + pltpu.roll(after, n + 7, 0)[:n, :]
+        )
+        out_ref[0, pl.ds(start, n), :] = total.astype(jnp.bfloat16)
+
+    def dots(value, tap):
+        return [
+            jnp.dot(value, weight[tap, b], preferred_element_type=jnp.float32) for b in range(3)
+        ]
+
+    def step(k, _):
+        @pl.when(k < n_chunks)
+        def _():
+            x_copy(k).wait_recv()
+            y_copy(k).start()
+
+            @pl.when(k == edge_chunk)
+            def _():
+                edge_copy(1).start()
+
+            first = dots(own[part(k), :], 1)
+            second = dots(arrived[0, part(k), :], x_tap)
+            for b in range(3):
+                sums[b, pl.ds(pl.multiple_of(EDGE + k * chunk, EDGE), chunk), :] = first[b] + second[b]
+
+        @pl.when((k >= 1) & (k < n_chunks + 1))
+        def _():
+            y_copy(k - 1).wait_recv()
+
+            @pl.when(z_send)
+            def _():
+                z_copy(k - 1).start()
+
+        @pl.when(k >= 2)
+        def _():
+            at = k - 2
+
+            @pl.when(z_recv)
+            def _():
+                z_copy(at).wait_recv()
+
+            @pl.when(at == edge_chunk)
+            def _():
+                edge_copy(2).start()
+
+            third = dots(arrived[slot, part(at), :], other_tap)
+            for b in range(3):
+                here = pl.ds(pl.multiple_of(EDGE + at * chunk, EDGE), chunk)
+                sums[b, here, :] = sums[b, here, :] + third[b]
+
+            @pl.when(at >= 1)
+            def _():
+                emit(pl.multiple_of((at - 1) * chunk, chunk), chunk)
+
+        return 0
+
+    lax.fori_loop(0, n_chunks + 2, step, 0)
+
+    for j in range(3):
+        edge_copy(j).wait_recv()
+    tap_col = 2 - 2 * w
+    rim = (
+        jnp.dot(edges[0], weight[1, tap_col], preferred_element_type=jnp.float32)
+        + jnp.dot(edges[1], weight[x_tap, tap_col], preferred_element_type=jnp.float32)
+        + jnp.dot(edges[2], weight[other_tap, tap_col], preferred_element_type=jnp.float32)
+    )
+
+    @pl.when(w == 0)
+    def _():
+        sums[2, pl.ds(EDGE + length, EDGE), :] = rim
+
+    @pl.when(w == 1)
+    def _():
+        sums[0, pl.ds(0, EDGE), :] = rim
+        emit(0, EDGE)
+
+    emit(length - chunk, chunk)
+
+    @pl.when(w == 0)
+    def _():
+        key_copy.wait_send()
+
+    for j in range(3):
+        edge_copy(j).wait_send()
+
+    def drain(k, _):
+        x_copy(k).wait_send()
+        y_copy(k).wait_send()
+
+        @pl.when(z_send)
+        def _():
+            z_copy(k).wait_send()
+
+        return 0
+
+    lax.fori_loop(0, n_chunks, drain, 0)
+
+
+def fused(n_rows, left_feat, right_feat, refine_weight):
+    _, length, chans = left_feat.shape
+    size = math.gcd(length, 256)
+    chunk = math.gcd(size, 128)
+    n_chunks = length // chunk
+    bf16, f32 = jnp.bfloat16, jnp.float32
+    dma = pltpu.SemaphoreType.DMA
+    return pl.pallas_call(
+        functools.partial(kernel, n_rows, size, chunk),
+        out_shape=(
+            jax.ShapeDtypeStruct((1, length), f32),
+            jax.ShapeDtypeStruct((1, length, chans), bf16),
+        ),
+        in_specs=[pl.BlockSpec(memory_space=pl.ANY)] * 3,
+        out_specs=[pl.BlockSpec(memory_space=pltpu.VMEM)] * 2,
+        scratch_shapes=[
+            pltpu.VMEM((length, chans), bf16),
+            pltpu.VMEM((2 * length, chans), bf16),
+            pltpu.VMEM((3, 3, chans, chans), bf16),
+            pltpu.VMEM((size, 2 * length), f32),
+            pltpu.VMEM((length, chans), bf16),
+            pltpu.VMEM((3, length, chans), bf16),
+            pltpu.VMEM((3, EDGE, chans), bf16),
+            pltpu.VMEM((3, length + 2 * EDGE, chans), f32),
+            dma((3,)),
+            dma((2, 1)),
+            dma((2, n_chunks)),
+            dma((2, n_chunks)),
+            dma((2, n_chunks)),
+            dma((2, 3)),
+        ],
+        compiler_params=pltpu.CompilerParams(collective_id=0, has_side_effects=True),
+    )(left_feat, right_feat, refine_weight)
+
+
 def solution(mesh):
+    n_rows, n_width = mesh.shape["rows"], mesh.shape["width"]
+
+    def local(left_feat, right_feat, refine_weight):
+        rows_here, length, chans = left_feat.shape
+        fits = n_rows % 4 == 0 and n_width == 2 and rows_here == 1
+        if fits and length % LANES == 0 and chans % LANES == 0:
+            return fused(n_rows, left_feat, right_feat, refine_weight)
+        return body(left_feat, right_feat, refine_weight)
+
     placed = (P("rows", "width", None), P("rows", "width", None), P())
     return jax.shard_map(
-        body,
+        local,
         mesh=mesh,
         in_specs=placed,
         out_specs=(P("rows", "width"), P("rows", "width", None)),

time: 82.2 us -> 35.4 us (0.43)
  the two profiles are of different devices: /device:TPU:0 before, /device:TPU:7 now
where the time goes in v1:
time: 35.4 us; the launch traced here: 34.7 us
  Pallas kernels  31 us (88%)
  local copies, waits for them, and re-layouts  3.13 us (9%)
  between operations  0.64 us (2%)
    pallas_call x1, Pallas kernels, fused(): pl.pallas_call(functools.partial(kernel, n_rows, size, chunk), out_shape=...  31 us
    unnamed x2, local copies, waits for them, and re-layouts  3.13 us

profile of v1, /device:TPU:7, one launch (start us, length us, event | category | flops | bytes accessed | tf_op | source)
XLA Modules:
  0.0 34.7 jit_solution(15371831012390432544)
XLA Ops:
  0.6 31.0 %shard_map.50 = (f32[1,1024]{1,0:T(1,128)}, bf16[1,1024,256]{2,1,0:T(8,128)(2,1)}) custom-call(bf16[1,1024,256]{2,1,0:T(8,128)(2,1)} %left_hbm.1, bf16[1,1024,256]{2,1,0:T(8,128)(2,1)} %right_hbm.1, bf16[3,3,256,256]{3,2,1,0:T(8,128)(2,1)} %weight_hbm.1), custom_call_target="tpu_custom_call" | custom-call | tf_op jit(solution)/shard_map/pallas_call | solution.py:374
  31.6 1.3 %copy.7 = f32[1,1024]{1,0:T(1,128)} copy(f32[1,1024]{1,0:T(1,128)} %get-tuple-element.4) | data formatting | bytes 8192
  32.9 1.9 %copy.8 = bf16[1,1024,256]{2,1,0:T(8,128)(2,1)} copy(bf16[1,1024,256]{2,1,0:T(8,128)(2,1)} %get-tuple-element.5) | data formatting | bytes 1048576

commit v2 on v1

--- a/solution.py
+++ b/solution.py
@@ -113,6 +113,10 @@
 MESH = pl.DeviceIdType.MESH
 EDGE = 16
 LANES = 128
+CHUNK = 128
+Y_LAG = 2
+Z_LAG = 4
+TILE_LAG = (9, 9)
 
 
 def attend(left, keys, scores, own, disp_ref, tile, first_key_tile, size):
@@ -238,19 +242,6 @@
     for load in loads:
         load.wait()
 
-    for side in (0, 1):
-
-        @pl.when(w == side)
-        def _():
-            if side == 1:
-                key_copy.wait_recv()
-            for tile in range(n_tiles):
-                attend(left, keys, scores, own, disp_ref, tile, side * n_tiles, size)
-                for k in range(tile * size // chunk, (tile + 1) * size // chunk):
-                    x_copy(k).start()
-
-    edge_copy(0).start()
-
     @pl.when(jnp.logical_not(z_recv))
     def _():
         arrived[2] = jnp.zeros((length, chans), jnp.bfloat16)
@@ -291,17 +282,17 @@
             for b in range(3):
                 sums[b, pl.ds(pl.multiple_of(EDGE + k * chunk, EDGE), chunk), :] = first[b] + second[b]
 
-        @pl.when((k >= 1) & (k < n_chunks + 1))
+        @pl.when((k >= Y_LAG) & (k < n_chunks + Y_LAG))
         def _():
-            y_copy(k - 1).wait_recv()
+            y_copy(k - Y_LAG).wait_recv()
 
             @pl.when(z_send)
             def _():
-                z_copy(k - 1).start()
-
-        @pl.when(k >= 2)
+                z_copy(k - Y_LAG).start()
+
+        @pl.when(k >= Z_LAG)
         def _():
-            at = k - 2
+            at = k - Z_LAG
 
             @pl.when(z_recv)
             def _():
@@ -322,7 +313,25 @@
 
         return 0
 
-    lax.fori_loop(0, n_chunks + 2, step, 0)
+    per_tile = size // chunk
+    for side in (0, 1):
+
+        @pl.when(w == side)
+        def _():
+            done = 0
+            if side == 1:
+                key_copy.wait_recv()
+            for tile in range(n_tiles):
+                attend(left, keys, scores, own, disp_ref, tile, side * n_tiles, size)
+                for k in range(tile * per_tile, (tile + 1) * per_tile):
+                    x_copy(k).start()
+                if tile == (1 - side) * (n_tiles - 1):
+                    edge_copy(0).start()
+                ready = max((tile - TILE_LAG[side]) * per_tile, done)
+                if ready > done:
+                    lax.fori_loop(done, ready, step, 0)
+                done = ready
+            lax.fori_loop(done, n_chunks + Z_LAG, step, 0)
 
     for j in range(3):
         edge_copy(j).wait_recv()
@@ -364,14 +373,19 @@
     lax.fori_loop(0, n_chunks, drain, 0)
 
 
+def hand_on(disp_in, out_in, disp_ref, out_ref):
+    disp_ref[...] = disp_in[...]
+    out_ref[...] = out_in[...]
+
+
 def fused(n_rows, left_feat, right_feat, refine_weight):
     _, length, chans = left_feat.shape
     size = math.gcd(length, 256)
-    chunk = math.gcd(size, 128)
+    chunk = math.gcd(size, CHUNK)
     n_chunks = length // chunk
     bf16, f32 = jnp.bfloat16, jnp.float32
     dma = pltpu.SemaphoreType.DMA
-    return pl.pallas_call(
+    found = pl.pallas_call(
         functools.partial(kernel, n_rows, size, chunk),
         out_shape=(
             jax.ShapeDtypeStruct((1, length), f32),
@@ -397,6 +411,12 @@
         ],
         compiler_params=pltpu.CompilerParams(collective_id=0, has_side_effects=True),
     )(left_feat, right_feat, refine_weight)
+    return pl.pallas_call(
+        hand_on,
+        out_shape=tuple(jax.ShapeDtypeStruct(one.shape, one.dtype) for one in found),
+        in_specs=[pl.BlockSpec(memory_space=pltpu.VMEM)] * 2,
+        out_specs=[pl.BlockSpec(memory_space=pltpu.VMEM)] * 2,
+    )(*found)
 
 
 def solution(mesh):

time: 35.4 us -> 28.3 us (0.80); the launches traced: 34.7 us -> 28.1 us
  Pallas kernels: 31 us -> 27.5 us
  local copies, waits for them, and re-layouts: 3.13 us -> 0 us
    pallas_call x1, Pallas kernels: 31 us -> 25.6 us  [fused(): pl.pallas_call(functools.partial(kernel, n_rows, size, chunk), out_shape=...]
    unnamed x2 -> x0, local copies, waits for them, and re-layouts: 3.13 us -> none
    pallas_call x0 -> x1, Pallas kernels: none -> 1.88 us  [fused(): pl.pallas_call(hand_on, out_shape=tuple((jax.ShapeDtypeStruct(one.shape,...]
where the time goes in v2:
time: 28.3 us; the launch traced here: 28.1 us
  Pallas kernels  27.5 us (97%)
  between operations  0.64 us (2%)
    pallas_call x1, Pallas kernels, fused(): pl.pallas_call(functools.partial(kernel, n_rows, size, chunk), out_shape=...  25.6 us
    pallas_call x1, Pallas kernels, fused(): pl.pallas_call(hand_on, out_shape=tuple((jax.ShapeDtypeStruct(one.shape,...  1.88 us

profile of v2, /device:TPU:7, one launch (start us, length us, event | category | flops | bytes accessed | tf_op | source)
XLA Modules:
  0.0 28.1 jit_solution(7591232171326649698)
XLA Ops:
  0.6 25.6 %shard_map.50 = (f32[1,1024]{1,0:T(1,128)}, bf16[1,1024,256]{2,1,0:T(8,128)(2,1)}) custom-call(bf16[1,1024,256]{2,1,0:T(8,128)(2,1)} %left_hbm.1, bf16[1,1024,256]{2,1,0:T(8,128)(2,1)} %right_hbm.1, bf16[3,3,256,256]{3,2,1,0:T(8,128)(2,1)} %weight_hbm.1), custom_call_target="tpu_custom_call" | custom-call | tf_op jit(solution)/shard_map/pallas_call | solution.py:388
  26.2 1.9 %shard_map.51 = (f32[1,1024]{1,0:T(1,128)}, bf16[1,1024,256]{2,1,0:T(8,128)(2,1)}) custom-call(f32[1,1024]{1,0:T(1,128)} %get-tuple-element.4.disp_in, bf16[1,1024,256]{2,1,0:T(8,128)(2,1)} %get-tuple-element.5.out_in), custom_call_target="tpu_custom_call" | custom-call | tf_op jit(solution)/shard_map/pallas_call | solution.py:414

commit v3 on v2

--- a/solution.py
+++ b/solution.py
@@ -113,9 +113,9 @@
 MESH = pl.DeviceIdType.MESH
 EDGE = 16
 LANES = 128
-CHUNK = 128
-Y_LAG = 2
-Z_LAG = 4
+CHUNK = 64
+Y_LAG = 6
+Z_LAG = 12
 TILE_LAG = (9, 9)
 
 
@@ -190,7 +190,7 @@
         pltpu.make_async_copy(right_hbm.at[0], keys.at[pl.ds(w * length, length)], load_sem.at[1]),
         pltpu.make_async_copy(weight_hbm, weight, load_sem.at[2]),
     ]
-    for load in loads:
+    for load in loads[:2]:
         load.start()
 
     barrier = pltpu.get_barrier_semaphore()
@@ -239,8 +239,9 @@
     def _():
         key_copy.start()
 
-    for load in loads:
+    for load in loads[:2]:
         load.wait()
+    loads[2].start()
 
     @pl.when(jnp.logical_not(z_recv))
     def _():
@@ -327,6 +328,8 @@
                     x_copy(k).start()
                 if tile == (1 - side) * (n_tiles - 1):
                     edge_copy(0).start()
+                if tile == 0:
+                    loads[2].wait()
                 ready = max((tile - TILE_LAG[side]) * per_tile, done)
                 if ready > done:
                     lax.fori_loop(done, ready, step, 0)

time: 28.3 us -> 28.3 us (level)
  no operation moved by 1% of the time
where the time goes in v3:
time: 28.3 us; the launch traced here: 28.1 us
  Pallas kernels  27.5 us (97%)
  between operations  0.64 us (2%)
    pallas_call x1, Pallas kernels, fused(): pl.pallas_call(functools.partial(kernel, n_rows, size, chunk), out_shape=...  25.6 us
    pallas_call x1, Pallas kernels, fused(): pl.pallas_call(hand_on, out_shape=tuple((jax.ShapeDtypeStruct(one.shape,...  1.88 us

profile of v3, /device:TPU:7, one launch (start us, length us, event | category | flops | bytes accessed | tf_op | source)
XLA Modules:
  0.0 28.1 jit_solution(7249463924355274493)
XLA Ops:
  0.6 25.6 %shard_map.50 = (f32[1,1024]{1,0:T(1,128)}, bf16[1,1024,256]{2,1,0:T(8,128)(2,1)}) custom-call(bf16[1,1024,256]{2,1,0:T(8,128)(2,1)} %left_hbm.1, bf16[1,1024,256]{2,1,0:T(8,128)(2,1)} %right_hbm.1, bf16[3,3,256,256]{3,2,1,0:T(8,128)(2,1)} %weight_hbm.1), custom_call_target="tpu_custom_call" | custom-call | tf_op jit(solution)/shard_map/pallas_call | solution.py:391
  26.2 1.9 %shard_map.51 = (f32[1,1024]{1,0:T(1,128)}, bf16[1,1024,256]{2,1,0:T(8,128)(2,1)}) custom-call(f32[1,1024]{1,0:T(1,128)} %get-tuple-element.4.disp_in, bf16[1,1024,256]{2,1,0:T(8,128)(2,1)} %get-tuple-element.5.out_in), custom_call_target="tpu_custom_call" | custom-call | tf_op jit(solution)/shard_map/pallas_call | solution.py:417
